TPU v7x, 32 devices: a whole 2x2x4 slice. The times are simulated.
32 devices in a mesh: dp: 8 (over z, y), tensor: 4 (over x, core).
Axes of the slice: x: 2, y: 2, z: 4, core: 2. Of those that a mesh axis runs over, the one named last changes fastest.
Arguments:
- tokens: bfloat16 [16384, 768], P(('dp', 'tensor')), may hold values from -6 to 6
- cotangent: bfloat16 [16384, 768], P(('dp', 'tensor')), may hold values from -6 to 6
- qkv_weight: float32 [3, 768, 768], P(None, 'dp', 'tensor'), may hold values from -0.21875 to 0.21875
- qv_bias: float32 [2, 768], P(None, 'tensor'), may hold values from -1.8 to 1.8
- out_weight: float32 [768, 768], P('tensor', 'dp'), may hold values from -1 to 1
- out_bias: float32 [768], replicated, may hold values from -1.8 to 1.8
- first_gain: float32 [768], replicated, may hold values from 0.5 to 1.5
- first_shift: float32 [768], replicated, may hold values from -1.2 to 1.2
- up_weight: float32 [768, 3072], P('dp', 'tensor'), may hold values from -0.21875 to 0.21875
- up_bias: float32 [3072], P('tensor'), may hold values from -1.8 to 1.8
- down_weight: float32 [3072, 768], P('tensor', 'dp'), may hold values from -0.109375 to 0.109375
- down_bias: float32 [768], replicated, may hold values from -1.8 to 1.8
- second_gain: float32 [768], replicated, may hold values from 0.5 to 1.5
- second_shift: float32 [768], replicated, may hold values from -1.2 to 1.2
- act_ranges: float32 [4], replicated, may hold values from 0.5 to 3.5, as said below
- long_lengths: int32 [8], P('dp'), may hold values from 128 to 512, as said below
- short_lengths: int32 [96], P('dp'), may hold values from 32 to 128, as said below
Outputs:
- layer_out: bfloat16 [16384, 768], P(('dp', 'tensor'))
- tokens_grad: bfloat16 [16384, 768], P(('dp', 'tensor'))
- qkv_grad: float32 [3, 768, 768], P(None, 'dp', 'tensor')
- qv_bias_grad: float32 [2, 768], P(None, 'tensor')
- out_grad: float32 [768, 768], P('tensor', 'dp')
- out_bias_grad: float32 [768], replicated
- first_gain_grad: float32 [768], replicated
- first_shift_grad: float32 [768], replicated
- up_grad: float32 [768, 3072], P('dp', 'tensor')
- up_bias_grad: float32 [3072], P('tensor')
- down_grad: float32 [3072, 768], P('tensor', 'dp')
- down_bias_grad: float32 [768], replicated
- second_gain_grad: float32 [768], replicated
- second_shift_grad: float32 [768], replicated
- new_ranges: float32 [4], replicated
Inputs may be any that keep to these rules, and one draw needn't show every extreme that they name: Each long sequence uses its first long_lengths slots; at least a quarter of 512, and some sequence uses all 512. Each short sequence uses its first short_lengths slots; at least a quarter of 128, and some sequence uses all 128. `act_ranges`: entry 1 lies in 0.5 to 0.8, the others in 2.5 to 3.5.
All inputs are finite; a program needn't handle non-finite values.
Results may differ from a plain program's by a relative error of at most 0.018.
The roundings to bfloat16 on the way count: a program that leaves them out, or rounds other values in their place, can miss the bound.
Values may be sent and summed in bfloat16 or wider, within the bound.
No kernel may reach another device: no remote copies, remote signals or barrier semaphores. Data moves between devices by JAX's collectives and lax.ppermute only.
A program may use at most 128 MiB of HBM per device.

v0:
```python
import jax
import jax.numpy as jnp
from jax import lax
from jax.sharding import PartitionSpec as P

HEAD_DIM = 64
LONG_LEN = 512
SHORT_LEN = 128
ema_decay = 0.9
epsilon = 1e-06
root_half = 0.7071067811865476
density_scale = 0.3989422804014327


def matmul_plain(left, right):
    return jnp.dot(left, right, preferred_element_type=jnp.float32)


def matmul_left_t(left, right):
    return lax.dot_general(
        left, right, (((0,), (0,)), ((), ())), preferred_element_type=jnp.float32
    )


def matmul_right_t(left, right):
    return lax.dot_general(
        left, right, (((1,), (1,)), ((), ())), preferred_element_type=jnp.float32
    )


def saturate(values, limit):
    return limit * jnp.tanh(values / limit)


def saturate_slope(values, limit):
    bent = jnp.tanh(values / limit)
    return 1.0 - bent * bent


def block_masks(long_part, short_part):
    per_block = LONG_LEN // SHORT_LEN
    position = jnp.arange(LONG_LEN, dtype=jnp.int32)
    long_segment = jnp.zeros((long_part.shape[0], LONG_LEN), jnp.int32)
    long_valid = position[None, :] < long_part[:, None]
    short_rows = short_part.reshape(-1, per_block)
    short_segment = jnp.broadcast_to(position // SHORT_LEN, (short_rows.shape[0], LONG_LEN))
    short_limit = jnp.repeat(short_rows, SHORT_LEN, axis=1)
    short_valid = (position % SHORT_LEN)[None, :] < short_limit
    return (
        jnp.concatenate([long_segment, short_segment], 0),
        jnp.concatenate([long_valid, short_valid], 0),
    )


def layer_norm_fwd(summed, gain, shift):
    average = jnp.mean(summed, axis=-1, keepdims=True)
    centered = summed - average
    inv_scale = lax.rsqrt(jnp.mean(centered * centered, axis=-1, keepdims=True) + epsilon)
    normed = centered * inv_scale
    return (normed * gain + shift, normed, inv_scale)


def norm_backward(incoming, normed, inv_scale, gain):
    scaled = incoming * gain
    row_mean = jnp.mean(scaled, axis=-1, keepdims=True)
    row_cross = jnp.mean(scaled * normed, axis=-1, keepdims=True)
    grad_in = inv_scale * (scaled - row_mean - normed * row_cross)
    return (grad_in, jnp.sum(incoming * normed, axis=0), jnp.sum(incoming, axis=0))


def gelu_slope(values):
    return (
        0.5 * (1.0 + lax.erf(values * root_half))
        + values * jnp.exp(-0.5 * values * values) * density_scale
    )


def score_block(queries, key_rows, segment, key_valid):
    scores = jnp.einsum(
        "qhd,khd->hqk", queries, key_rows, preferred_element_type=jnp.float32
    ) * HEAD_DIM ** (-0.5)
    allowed = (segment[:, None] == segment[None, :]) & key_valid[None, :]
    return jnp.where(allowed[None, :, :], scores, -1000000000.0)


def block_forward(pieces):
    queries, key_rows, values, segment, key_valid = pieces
    scores = score_block(queries, key_rows, segment, key_valid)
    row_max = jnp.max(scores, axis=-1, keepdims=True)
    expanded = jnp.exp(scores - row_max)
    row_total = jnp.sum(expanded, axis=-1, keepdims=True)
    shares = (expanded / row_total).astype(jnp.bfloat16)
    context = jnp.einsum("hqk,khd->qhd", shares, values, preferred_element_type=jnp.float32)
    return (context, (row_max + jnp.log(row_total))[:, :, 0])


def block_backward(pieces):
    queries, key_rows, values, segment, key_valid, log_total, grad_ctx = pieces
    score_scale = HEAD_DIM ** (-0.5)
    scores = score_block(queries, key_rows, segment, key_valid)
    shares = jnp.exp(scores - log_total[:, :, None])
    grad_shares = jnp.einsum("qhd,khd->hqk", grad_ctx, values, preferred_element_type=jnp.float32)
    row_inner = jnp.sum(shares * grad_shares, axis=-1, keepdims=True)
    grad_scores = (shares * (grad_shares - row_inner)).astype(jnp.bfloat16)
    grad_values = jnp.einsum(
        "hqk,qhd->khd", shares.astype(jnp.bfloat16), grad_ctx, preferred_element_type=jnp.float32
    )
    grad_queries = (
        jnp.einsum("hqk,khd->qhd", grad_scores, key_rows, preferred_element_type=jnp.float32)
        * score_scale
    )
    grad_keys = (
        jnp.einsum("hqk,qhd->khd", grad_scores, queries, preferred_element_type=jnp.float32)
        * score_scale
    )
    return (
        grad_queries.astype(jnp.bfloat16),
        grad_keys.astype(jnp.bfloat16),
        grad_values.astype(jnp.bfloat16),
    )


def body(
    tokens,
    cotangent,
    qkv_weight,
    qv_bias,
    out_weight,
    out_bias,
    first_gain,
    first_shift,
    up_weight,
    up_bias,
    down_weight,
    down_bias,
    second_gain,
    second_shift,
    act_ranges,
    long_lengths,
    short_lengths,
):
    tensor_lanes = lax.axis_size("tensor")
    column = lax.axis_index("tensor")
    shard_rows = tokens.shape[0]
    group_rows = shard_rows * tensor_lanes
    head_cols = qkv_weight.shape[2]
    up_cols = up_weight.shape[1]
    blocked = (group_rows // LONG_LEN, LONG_LEN, head_cols // HEAD_DIM, HEAD_DIM)
    masters = (
        qkv_weight.astype(jnp.bfloat16),
        out_weight.astype(jnp.bfloat16),
        up_weight.astype(jnp.bfloat16),
        down_weight.astype(jnp.bfloat16),
    )
    qkv_full, out_full, up_full, down_full = (
        lax.all_gather(masters[0], "dp", axis=1, tiled=True),
        lax.all_gather(masters[1], "dp", axis=1, tiled=True),
        lax.all_gather(masters[2], "dp", axis=0, tiled=True),
        lax.all_gather(masters[3], "dp", axis=1, tiled=True),
    )
    inputs = tokens.astype(jnp.float32)
    in_clip = jnp.clip(inputs, -act_ranges[0], act_ranges[0]).astype(jnp.bfloat16)
    in_rows = lax.all_gather(in_clip, "tensor", axis=0, tiled=True)
    projected = jnp.einsum("td,jde->jte", in_rows, qkv_full, preferred_element_type=jnp.float32)
    queries = (projected[0] + qv_bias[0]).astype(jnp.bfloat16).reshape(blocked)
    key_rows = projected[1].astype(jnp.bfloat16).reshape(blocked)
    values = (projected[2] + qv_bias[1]).astype(jnp.bfloat16).reshape(blocked)
    segment, key_valid = block_masks(long_lengths, short_lengths)
    context, log_total = lax.map(block_forward, (queries, key_rows, values, segment, key_valid))
    context = context.reshape(group_rows, head_cols)
    ctx_clip = saturate(context, act_ranges[1]).astype(jnp.bfloat16)
    attn_sum = lax.psum_scatter(
        matmul_plain(ctx_clip, out_full).astype(jnp.bfloat16),
        "tensor",
        scatter_dimension=0,
        tiled=True,
    ).astype(jnp.float32)
    first_sum = inputs + attn_sum + out_bias
    middle, first_normed, first_inv = layer_norm_fwd(first_sum, first_gain, first_shift)
    mid_clip = saturate(middle, act_ranges[2]).astype(jnp.bfloat16)
    mid_rows = lax.all_gather(mid_clip, "tensor", axis=0, tiled=True)
    up_out = matmul_plain(mid_rows, up_full) + up_bias
    hidden = jax.nn.gelu(up_out, approximate=False)
    act_clip = saturate(hidden, act_ranges[3]).astype(jnp.bfloat16)
    ffn_sum = lax.psum_scatter(
        matmul_plain(act_clip, down_full).astype(jnp.bfloat16),
        "tensor",
        scatter_dimension=0,
        tiled=True,
    ).astype(jnp.float32)
    second_sum = middle + ffn_sum + down_bias
    layer_out, second_normed, second_inv = layer_norm_fwd(second_sum, second_gain, second_shift)
    maxima = lax.pmax(
        (
            jnp.max(jnp.abs(inputs)),
            jnp.max(jnp.abs(context)),
            jnp.max(jnp.abs(middle)),
            jnp.max(jnp.abs(hidden)),
        ),
        ("dp", "tensor"),
    )
    new_ranges = ema_decay * act_ranges + (1.0 - ema_decay) * jnp.stack(maxima)
    grad_second, second_gain_part, second_shift_part = norm_backward(
        cotangent.astype(jnp.float32), second_normed, second_inv, second_gain
    )
    down_rows = lax.all_gather(grad_second.astype(jnp.bfloat16), "tensor", axis=0, tiled=True)
    qkv_back, out_back, up_back, down_back = (
        lax.all_gather(masters[0], "dp", axis=1, tiled=True),
        lax.all_gather(masters[1], "dp", axis=1, tiled=True),
        lax.all_gather(masters[2], "dp", axis=0, tiled=True),
        lax.all_gather(masters[3], "dp", axis=1, tiled=True),
    )
    down_grad = matmul_left_t(act_clip, down_rows)
    grad_act = matmul_right_t(down_rows, down_back) * saturate_slope(hidden, act_ranges[3])
    grad_up = (grad_act * gelu_slope(up_out)).astype(jnp.bfloat16)
    up_grad = matmul_left_t(mid_rows, grad_up)
    mid_sum = lax.psum_scatter(
        matmul_right_t(grad_up, up_back).astype(jnp.bfloat16),
        "tensor",
        scatter_dimension=0,
        tiled=True,
    ).astype(jnp.float32)
    grad_middle = grad_second + mid_sum * saturate_slope(middle, act_ranges[2])
    grad_first, first_gain_part, first_shift_part = norm_backward(
        grad_middle, first_normed, first_inv, first_gain
    )
    attn_rows = lax.all_gather(grad_first.astype(jnp.bfloat16), "tensor", axis=0, tiled=True)
    out_grad = matmul_left_t(ctx_clip, attn_rows)
    grad_ctx = (
        matmul_right_t(attn_rows, out_back) * saturate_slope(context, act_ranges[1])
    ).astype(jnp.bfloat16)
    grad_queries, grad_keys, grad_values = lax.map(
        block_backward,
        (queries, key_rows, values, segment, key_valid, log_total, grad_ctx.reshape(blocked)),
    )
    stacked = jnp.stack(
        [
            grad_queries.reshape(group_rows, head_cols),
            grad_keys.reshape(group_rows, head_cols),
            grad_values.reshape(group_rows, head_cols),
        ]
    )
    qkv_grad = jnp.einsum("td,jte->jde", in_rows, stacked, preferred_element_type=jnp.float32)
    input_sum = lax.psum_scatter(
        jnp.einsum("jte,jde->td", stacked, qkv_back, preferred_element_type=jnp.float32).astype(
            jnp.bfloat16
        ),
        "tensor",
        scatter_dimension=0,
        tiled=True,
    ).astype(jnp.float32)
    tokens_grad = (grad_first + jnp.where(jnp.abs(inputs) <= act_ranges[0], input_sum, 0.0)).astype(
        jnp.bfloat16
    )
    qkv_grad, out_grad, up_grad, down_grad = (
        lax.psum_scatter(qkv_grad, "dp", scatter_dimension=1, tiled=True),
        lax.psum_scatter(out_grad, "dp", scatter_dimension=1, tiled=True),
        lax.psum_scatter(up_grad, "dp", scatter_dimension=0, tiled=True),
        lax.psum_scatter(down_grad, "dp", scatter_dimension=1, tiled=True),
    )
    lane_hot = (jnp.arange(tensor_lanes) == column).astype(jnp.float32)

    def spread(vector_piece):
        return (lane_hot[:, None] * vector_piece[None, :]).reshape(-1)

    query_bias_part = jnp.sum(stacked[0].astype(jnp.float32), axis=0)
    value_bias_part = jnp.sum(stacked[2].astype(jnp.float32), axis=0)
    up_bias_part = jnp.sum(grad_up.astype(jnp.float32), axis=0)
    shared = jnp.stack(
        [
            jnp.sum(grad_first, axis=0),
            first_gain_part,
            first_shift_part,
            jnp.sum(grad_second, axis=0),
            second_gain_part,
            second_shift_part,
        ]
    )
    query_total, value_total, up_total, shared_total = lax.psum(
        (spread(query_bias_part), spread(value_bias_part), spread(up_bias_part), shared),
        ("dp", "tensor"),
    )
    qv_bias_grad = jnp.stack(
        [
            lax.dynamic_slice_in_dim(query_total, column * head_cols, head_cols),
            lax.dynamic_slice_in_dim(value_total, column * head_cols, head_cols),
        ]
    )
    up_bias_grad = lax.dynamic_slice_in_dim(up_total, column * up_cols, up_cols)
    return (
        layer_out.astype(jnp.bfloat16),
        tokens_grad,
        qkv_grad,
        qv_bias_grad,
        out_grad,
        shared_total[0],
        shared_total[1],
        shared_total[2],
        up_grad,
        up_bias_grad,
        down_grad,
        shared_total[3],
        shared_total[4],
        shared_total[5],
        new_ranges,
    )


def solution(mesh):
    in_specs = (
        P(("dp", "tensor"), None),
        P(("dp", "tensor"), None),
        P(None, "dp", "tensor"),
        P(None, "tensor"),
        P("tensor", "dp"),
        P(),
        P(),
        P(),
        P("dp", "tensor"),
        P("tensor"),
        P("tensor", "dp"),
        P(),
        P(),
        P(),
        P(),
        P("dp"),
        P("dp"),
    )
    out_specs = (
        P(("dp", "tensor"), None),
        P(("dp", "tensor"), None),
        P(None, "dp", "tensor"),
        P(None, "tensor"),
        P("tensor", "dp"),
        P(),
        P(),
        P(),
        P("dp", "tensor"),
        P("tensor"),
        P("tensor", "dp"),
        P(),
        P(),
        P(),
        P(),
    )
    return jax.shard_map(body, mesh=mesh, in_specs=in_specs, out_specs=out_specs, check_vma=False)
```

profile of v0, /device:TPU:0, one launch (start us, length us, event | category | flops | bytes accessed | tf_op | source)
XLA Modules:
  0.0 788.6 jit_solution(17839399608265176750)
XLA Ops:
  10.0 2.8 fusion.80
  14.0 38.9 %all_gather.29 = bf16[3,768,192]{2,0,1:T(4,128)(2,1)S(1)} all-gather(bf16[3,96,192]{2,0,1:T(4,128)(2,1)S(1)} %copy.88), channel_id=1, replica_groups=mesh['dp'=8,'tensor'=4] {'dp'}, dimensions={1}, use_global_device_ids=true | all-gather | bytes 995328 | tf_op jit(solution)/shard_map/all_gather | solution.py:156
  52.9 2.0 copy.89
  56.7 31.1 %all_gather.30 = bf16[192,768]{0,1:T(8,128)(2,1)S(1)} all-gather(bf16[192,96]{0,1:T(8,128)(2,1)S(1)} %copy.94), channel_id=1, replica_groups=mesh['dp'=8,'tensor'=4] {'dp'}, dimensions={1}, use_global_device_ids=true | all-gather | bytes 331776 | tf_op jit(solution)/shard_map/all_gather | solution.py:157
  87.7 4.1 fusion.104
  93.3 3.2 squeeze.75
  96.5 2.2 squeeze.76
  99.4 2.9 fusion.83
  102.4 16.9 %while.26 = (s32[]{:T(128)}, f32[4,512,3,64]{1,3,2,0:T(8,128)}, f32[4,3,512]{2,1,0:T(4,128)}, bf16[4,512,3,64]{1,3,2,0:T(8,128)(2,1)S(1)}, s32[4,512]{1,0:T(4,12...) while((s32[]{:T(128)}, f32[4,512,3,64]{1,3,2,0:T(8,128)}, ...), condition=%wide.region_3.4_spmd, body=%wide.region_0.3_spmd.sunk | while | flops 211286528 | bytes 11534437 | solution.py:169
  104.8 1.8 fusion.151
  113.2 1.8 fusion.151
  119.3 4.2 abs_reduce_fusion.2
  125.2 2.7 convolution_convert_fusion.2
  128.9 36.0 %reduce-scatter.13.cloned.1.call-done = bf16[512,768]{1,0:T(8,128)(2,1)} async-done(((bf16[2048,768]{1,0:T(8,128)(2,1)}), bf16[512,768]{1,0:T(8,128)(2,1)}) %reduce-scatter.13.cloned.1.call-update) | async-done | bytes 786448 | tf_op jit(solution)/shard_map/reduce_scatter | solution.py:172
  168.7 2.9 multiply_convert_fusion.2
  173.4 27.0 %all-gather.9.cloned.1.call-done = bf16[2048,768]{1,0:T(8,128)(2,1)} async-done(((bf16[512,768]{1,0:T(8,128)(2,1)}), bf16[2048,768]{1,0:T(8,128)(2,1)}) %all-gather.9.cloned.1.call-update) | async-done | bytes 3145744 | tf_op jit(solution)/shard_map/all_gather | solution.py:181
  200.4 17.9 %abs_reduce_fusion = (f32[]{:T(128)}, f32[2048,768]{1,0:T(8,128)S(1)}, f32[2048,768]{1,0:T(8,128)}) fusion(f32[768]{0:T(1024)} %param.30, bf16[2048,768]{1,0:T(8,128)(2,1)} %all-gather.9.cloned.1.call-done, bf16[768,768]{1,0:T(8,128)(2,1)} %all-gather.11.cloned.1.call-done), kind=kOutput, calls=%fused_computation.74 | convolution fusion | flops 2521300992 | bytes 16911364 | tf_op jit(solution)/shard_map/dot_general | solution.py:16
  218.3 2.7 copy-done.5
  221.0 3.6 multiply_convert_fusion.1
  224.6 19.9 %all-gather.13.cloned.1.call-done = bf16[768,768]{0,1:T(8,128)(2,1)} async-done(((bf16[768,96]{0,1:T(8,128)(2,1)}), bf16[768,768]{0,1:T(8,128)(2,1)}) %all-gather.13.cloned.1.call-update) | async-done | bytes 1179664 | tf_op jit(solution)/shard_map/all_gather | solution.py:159
  244.5 6.5 convolution_convert_fusion.1
  251.5 35.7 %reduce-scatter.15.cloned.1.call-done = bf16[512,768]{1,0:T(8,128)(2,1)} async-done(((bf16[2048,768]{1,0:T(8,128)(2,1)}), bf16[512,768]{1,0:T(8,128)(2,1)}) %reduce-scatter.15.cloned.1.call-update) | async-done | bytes 786448 | tf_op jit(solution)/shard_map/reduce_scatter | solution.py:185
  287.2 2.0 fusion.101
  290.9 2.1 fusion.98
  295.3 28.6 %all-gather.15.cloned.1.call-done = bf16[2048,768]{1,0:T(8,128)(2,1)} async-done(((bf16[512,768]{1,0:T(8,128)(2,1)}), bf16[2048,768]{1,0:T(8,128)(2,1)}) %all-gather.15.cloned.1.call-update) | async-done | bytes 3145744 | tf_op jit(solution)/shard_map/all_gather | solution.py:206
  323.9 11.1 %convert_reduce_fusion = (f32[768]{0:T(1024)}, bf16[2048,768]{1,0:T(8,128)(2,1)S(1)}) fusion(f32[2048,768]{1,0:T(8,128)} %get-tuple-element.347, f32[768]{0:T(1024)} %param.30, f32[2048,768]{1,0:T(8,128)} %copy-done.5, f32[]{:T(128)} %bitcast.27, bf16[2048,768]{1,0:T(8,128)(2,1)} %all-gather.15.cloned.1.call-done, ...), kind=kOutput, calls=%fused_computation.75 | convolution fusion | flops 2442657024 | bytes 20060164 | tf_op jit(solution)/shard_map/dot_general | solution.py:26
  336.7 4.0 convolution_convert_fusion
  340.8 37.8 %reduce-scatter.17.cloned.1.call-done = bf16[512,768]{1,0:T(8,128)(2,1)} async-done(((bf16[2048,768]{1,0:T(8,128)(2,1)}), bf16[512,768]{1,0:T(8,128)(2,1)}) %reduce-scatter.17.cloned.1.call-update) | async-done | bytes 786448 | tf_op jit(solution)/shard_map/reduce_scatter | solution.py:217
  378.5 4.9 multiply_reduce_fusion.1
  383.5 2.0 fusion.100
  388.0 2.4 copy.95
  392.1 24.2 %all-gather.17.cloned.1.call-done = bf16[2048,768]{1,0:T(8,128)(2,1)} async-done(((bf16[512,768]{1,0:T(8,128)(2,1)}), bf16[2048,768]{1,0:T(8,128)(2,1)}) %all-gather.17.cloned.1.call-update) | async-done | bytes 3145744 | tf_op jit(solution)/shard_map/all_gather | solution.py:227
  416.4 3.5 fusion.70
  422.7 32.6 %while.27 = (s32[]{:T(128)}, bf16[4,512,3,64]{1,3,2,0:T(8,128)(2,1)}, bf16[4,512,3,64]{1,3,2,0:T(8,128)(2,1)}, bf16[4,512,3,64]{1,3,2,0:T(8,128)(2,1)}, bf16[4,5...) while((s32[]{:T(128)}, ...), condition=%wide.region_17.18_spmd, body=%wide.region_15.17_spmd.sunk | while | flops 511408640 | bytes 26129024 | solution.py:232
  457.8 4.1 convolution_bitcast_fusion
  469.8 5.9 fusion.85
  475.6 4.3 copy.107
  479.9 4.8 reshape.286
  484.8 6.0 bitcast_convert_fusion
  490.9 7.0 fusion.106
  498.3 7.0 fusion.105
  505.5 39.8 %all-reduce.2 = (f32[1]{0:T(128)}, f32[1]{0:T(128)}, f32[1]{0:T(128)}, f32[1]{0:T(128)}) all-reduce(f32[1]{0:T(128)} %bitcast.37, f32[1]{0:T(128)} %bitcast.36, f32[1]{0:T(128)} %bitcast.35, f32[1]{0:T(128)} %bitcast.34), channel_id=1, replica_groups=mesh['dp'=8,'tensor'=4] {'dp','tensor'}, use_global_device_ids=true, to_apply=%region_43.44 | all-reduce | flops 4 | bytes 32 | tf_op jit(solution)/shard_map/pmax | solution.py:193
  545.4 3.2 fusion.96
  550.5 41.6 %all-reduce.1 = (f32[768]{0:T(1024)S(1)}, f32[768]{0:T(1024)S(1)}, f32[6,768]{1,0:T(8,128)S(1)}, f32[3072]{0:T(1024)S(1)}) all-reduce(f32[768]{0:T(1024)S(1)} %mul.303, f32[768]{0:T(1024)S(1)} %mul.298, f32[6,768]{1,0:T(8,128)S(1)} %stack.58, f32[3072]{0:T(1024)S(1)} %mul.309), channel_id=1, replica_groups=mesh['dp'=8,'tensor'=4] {'dp','tensor'}, use_global_device_ids=true, to_apply=%region_23.24 | all-reduce | flops 9216 | bytes 73728 | tf_op jit(solution)/shard_map/psum | solution.py:279
  597.7 36.6 %reduce-scatter.19.cloned.1.call-done = bf16[512,768]{1,0:T(8,128)(2,1)} async-done(((bf16[2048,768]{1,0:T(8,128)(2,1)}), bf16[512,768]{1,0:T(8,128)(2,1)}) %reduce-scatter.19.cloned.1.call-update) | async-done | bytes 786448 | tf_op jit(solution)/shard_map/reduce_scatter | solution.py:244
  634.3 2.9 add_convert_fusion
  637.2 70.8 %reduce-scatter.23.cloned.1.call-done = f32[768,96]{0,1:T(8,128)} async-done(((f32[768,768]{0,1:T(8,128)}), f32[768,96]{0,1:T(8,128)}) %reduce-scatter.23.cloned.1.call-update) | async-done | bytes 294928 | tf_op jit(solution)/shard_map/reduce_scatter | solution.py:259
  708.0 73.0 %reduce-scatter.21.cloned.1.call-done = f32[96,768]{1,0:T(8,128)} async-done(((f32[768,768]{1,0:T(8,128)}), f32[96,768]{1,0:T(8,128)}) %reduce-scatter.21.cloned.1.call-update) | async-done | bytes 294928 | tf_op jit(solution)/shard_map/reduce_scatter | solution.py:258
  (241 shorter events, 91.3 us)
Async XLA Ops:
  8.0 79.7 %all-gather.7.cloned.1.call-start = ((), (), s32[]{:S(2)}) async-start(), calls=%async_computation.8 | async-start | bytes 3932160 | tf_op jit(solution)/shard_map/all_gather | solution.py:163
  12.8 42.1 %copy-start.28 = (f32[2,192]{1,0:T(2,128)S(1)}, f32[2,192]{1,0:T(2,128)}, u32[]{:S(2)}) copy-start(f32[2,192]{1,0:T(2,128)} %param.24) | copy-start | bytes 4612
  12.8 42.9 %copy-start.29 = (s32[12]{0:T(128)S(1)}, s32[12]{0:T(128)}, u32[]{:S(2)}) copy-start(s32[12]{0:T(128)} %param.37) | copy-start | bytes 148
  12.8 43.7 %copy-start.14 = (f32[192,96]{1,0:T(8,128)S(1)}, f32[192,96]{1,0:T(8,128)}, u32[]{:S(2)}) copy-start(f32[192,96]{1,0:T(8,128)} %param.25) | copy-start | bytes 221188
  12.8 152.2 %reduce-scatter.13.cloned.1.call-start = ((), (), s32[]{:S(2)}) async-start(), calls=%async_computation.9 | async-start | bytes 3932160 | tf_op jit(solution)/shard_map/reduce_scatter | solution.py:172
  119.3 5.0 copy-start.6
  124.3 0.9 copy-start.8
  125.2 2.8 copy-start.12
  125.2 39.8 %copy-start = (bf16[512,768]{1,0:T(8,128)(2,1)S(1)}, bf16[512,768]{1,0:T(8,128)(2,1)}, u32[]{:S(2)}) copy-start(bf16[512,768]{1,0:T(8,128)(2,1)} %param.21) | copy-start | bytes 2359300
  125.2 39.8 %copy-start.13 = (f32[768]{0:T(1024)S(1)}, f32[768]{0:T(1024)}, u32[]{:S(2)}) copy-start(f32[768]{0:T(1024)} %param.26) | copy-start | bytes 9220
  127.9 45.5 %all-gather.11.cloned.1.call-start = ((), (), s32[]{:S(2)}) async-start(), calls=%async_computation.11 | async-start | bytes 1327104 | tf_op jit(solution)/shard_map/all_gather | solution.py:158
  128.7 71.7 %all-gather.9.cloned.1.call-start = ((), (), s32[]{:S(2)}) async-start(), calls=%async_computation.10 | async-start | bytes 3932160 | tf_op jit(solution)/shard_map/all_gather | solution.py:181
  165.0 3.7 copy-start.1
  166.5 1.6 copy-start.15
  168.1 0.6 copy-start.17
  171.6 72.9 %all-gather.13.cloned.1.call-start = ((), (), s32[]{:S(2)}) async-start(), calls=%async_computation.12 | async-start | bytes 1327104 | tf_op jit(solution)/shard_map/all_gather | solution.py:159
  173.3 113.9 %reduce-scatter.15.cloned.1.call-start = ((), (), s32[]{:S(2)}) async-start(), calls=%async_computation.13 | async-start | bytes 3932160 | tf_op jit(solution)/shard_map/reduce_scatter | solution.py:185
  218.3 2.7 copy-start.5
  251.0 72.9 %all-gather.15.cloned.1.call-start = ((), (), s32[]{:S(2)}) async-start(), calls=%async_computation.14 | async-start | bytes 3932160 | tf_op jit(solution)/shard_map/all_gather | solution.py:206
  287.2 2.3 copy-start.10
  287.2 2.3 copy-start.20
  287.2 3.7 copy-start.27
  293.0 1.2 copy-start.4
  295.2 83.3 %reduce-scatter.17.cloned.1.call-start = ((), (), s32[]{:S(2)}) async-start(), calls=%async_computation.15 | async-start | bytes 3932160 | tf_op jit(solution)/shard_map/reduce_scatter | solution.py:217
  323.9 12.7 %copy-start.30 = (bf16[768,768]{1,0:T(8,128)(2,1)S(1)}, bf16[768,768]{1,0:T(8,128)(2,1)}, u32[]{:S(2)}) copy-start(bf16[768,768]{1,0:T(8,128)(2,1)} %all-gather.11.cloned.1.call-done) | copy-start | bytes 3538948
  335.0 1.7 copy-start.31
  340.7 75.6 %all-gather.17.cloned.1.call-start = ((), (), s32[]{:S(2)}) async-start(), calls=%async_computation.16 | async-start | bytes 3932160 | tf_op jit(solution)/shard_map/all_gather | solution.py:227
  378.5 4.9 copy-start.16
  385.4 1.2 copy-start.2
  387.7 206.5 %reduce-scatter.27.cloned.1.call-start = ((), (), s32[]{:S(2)}) async-start(), calls=%async_computation.21 | async-start | bytes 884736
  455.4 2.4 copy-start.9
  461.9 133.9 %reduce-scatter.25.cloned.1.call-start = ((), (), s32[]{:S(2)}) async-start(), calls=%async_computation.20 | async-start | bytes 2211840
  479.9 4.9 copy-start.11
  484.7 149.6 %reduce-scatter.19.cloned.1.call-start = ((), (), s32[]{:S(2)}) async-start(), calls=%async_computation.17 | async-start | bytes 3932160 | tf_op jit(solution)/shard_map/reduce_scatter | solution.py:244
  490.8 217.2 %reduce-scatter.23.cloned.1.call-start = ((), (), s32[]{:S(2)}) async-start(), calls=%async_computation.19 | async-start | bytes 2654208 | tf_op jit(solution)/shard_map/reduce_scatter | solution.py:259
  497.9 7.5 copy-start.21
  497.9 7.5 copy-start.19
  497.9 7.5 copy-start.18
  497.9 7.5 copy-start.26
  497.9 47.4 %copy-start.24 = (f32[768]{0:T(1024)S(1)}, f32[768]{0:T(1024)}, u32[]{:S(2)}) copy-start(f32[768]{0:T(1024)} %get-tuple-element.326) | copy-start | bytes 9220
  497.9 47.4 %copy-start.23 = (f32[768]{0:T(1024)S(1)}, f32[768]{0:T(1024)}, u32[]{:S(2)}) copy-start(f32[768]{0:T(1024)} %get-tuple-element.258) | copy-start | bytes 9220
  497.9 47.4 %copy-start.22 = (f32[768]{0:T(1024)S(1)}, f32[768]{0:T(1024)}, u32[]{:S(2)}) copy-start(f32[768]{0:T(1024)} %get-tuple-element.264) | copy-start | bytes 9220
  498.0 47.4 %copy-start.25 = (f32[4]{0:T(128)S(1)}, f32[4]{0:T(128)}, u32[]{:S(2)}) copy-start(f32[4]{0:T(128)} %param.35) | copy-start | bytes 52
  498.0 50.6 %copy-start.7 = (bf16[4,512,3,64]{1,3,2,0:T(8,128)(2,1)S(1)}, bf16[4,512,3,64]{1,3,2,0:T(8,128)(2,1)}, u32[]{:S(2)}) copy-start(bf16[4,512,3,64]{1,3,2,0:T(8,128)(2,1)} %get-tuple-element.119) | copy-start | bytes 2359300
  498.0 283.1 %reduce-scatter.21.cloned.1.call-start = ((), (), s32[]{:S(2)}) async-start(), calls=%async_computation.18 | async-start | bytes 2654208 | tf_op jit(solution)/shard_map/reduce_scatter | solution.py:258
  505.3 129.0 %copy-start.3 = (f32[512,768]{1,0:T(8,128)S(1)}, f32[512,768]{1,0:T(8,128)}, u32[]{:S(2)}) copy-start(f32[512,768]{1,0:T(8,128)} %copy-done.2) | copy-start | bytes 4718596
Sparse Core Ops, SparseCore 0:
  12.9 31.2 all-gather.6
  128.0 36.8 reduce-scatter.12
  295.4 28.5 all-gather.14
  387.8 28.4 all-gather.16
Sparse Core Ops, SparseCore 1:
  131.2 40.4 all-gather.10
  173.6 26.7 all-gather.8
  203.0 41.4 all-gather.12
  251.1 36.1 reduce-scatter.14
  340.8 37.7 reduce-scatter.16
  462.0 63.3 reduce-scatter.26
  528.7 66.4 reduce-scatter.24
  597.6 36.7 reduce-scatter.18
  638.3 69.7 reduce-scatter.22
  712.1 68.9 reduce-scatter.20
where the time goes:
time: 799 us; the launch traced here: 789 us
  waiting for transfers between devices  390 us (49%)
  blocking collectives  151 us (19%)
  matrix products  116 us (15%)
  other arithmetic  56.4 us (7%)
  local copies, waits for them, and re-layouts  55.7 us (7%)
  between operations  17.5 us (2%)
    reduce_scatter x1, waiting for transfers between devices, body(): lax.psum_scatter(up_grad, 'dp', scatter_dimension=0, tiled=True)  73 us
    reduce_scatter x1, waiting for transfers between devices, body(): lax.psum_scatter(down_grad, 'dp', scatter_dimension=1, tiled=True)  70.8 us
    psum x1, blocking collectives, body(): lax.psum((spread(query_bias_part), spread(value_bias_part), spread(up_bia...  41.6 us
    pmax x1, blocking collectives, body(): lax.pmax((jnp.max(jnp.abs(inputs)), jnp.max(jnp.abs(context)), jnp.max(jn...  39.8 us
    all_gather x1, blocking collectives, body(): lax.all_gather(masters[0], 'dp', axis=1, tiled=True)  38.9 us
    reduce_scatter x1, waiting for transfers between devices, body(): lax.psum_scatter(matmul_right_t(grad_up, up_back).astype(jnp.bfloat16), '...  37.8 us
    reduce_scatter x1, waiting for transfers between devices, body(): lax.psum_scatter(jnp.einsum('jte,jde->td', stacked, qkv_back, preferred_e...  36.6 us
    reduce_scatter x1, waiting for transfers between devices, body(): lax.psum_scatter(matmul_plain(ctx_clip, out_full).astype(jnp.bfloat16), '...  36 us
  transfers between devices with their start and end apart: 14, of which 10 were waited for; matrix products, arithmetic and copies ran while one was open for 12% of the time, Pallas kernels for 0%

commit v1 on v0

--- a/solution.py
+++ b/solution.py
@@ -10,6 +10,19 @@
 epsilon = 1e-06
 root_half = 0.7071067811865476
 density_scale = 0.3989422804014327
+
+
+def ring_gather(x, axis, dim):
+    ways = lax.axis_size(axis)
+    up = [(d, (d + 1) % ways) for d in range(ways)]
+    down = [(d, (d - 1) % ways) for d in range(ways)]
+    earlier, later = ([x], [x])
+    for _ in range(ways // 2):
+        earlier.append(lax.ppermute(earlier[-1], axis, up))
+    for _ in range((ways - 1) // 2):
+        later.append(lax.ppermute(later[-1], axis, down))
+    line = jnp.concatenate([*earlier[::-1], *later[1:]], axis=dim)
+    return jnp.roll(line, (lax.axis_index(axis) - ways // 2) * x.shape[dim], axis=dim)
 
 
 def matmul_plain(left, right):
@@ -154,7 +167,7 @@
     )
     qkv_full, out_full, up_full, down_full = (
         lax.all_gather(masters[0], "dp", axis=1, tiled=True),
-        lax.all_gather(masters[1], "dp", axis=1, tiled=True),
+        ring_gather(masters[1], "dp", 1),
         lax.all_gather(masters[2], "dp", axis=0, tiled=True),
         lax.all_gather(masters[3], "dp", axis=1, tiled=True),
     )

time: 799 us -> 807 us (1.010)
  starting transfers between devices: 1.86 us -> 17.4 us
  waiting for transfers between devices: 390 us -> 380 us
    all_gather x1, waiting for transfers between devices: 24.2 us -> 0.01 us  [body(): lax.all_gather(grad_first.astype(jnp.bfloat16), 'tensor', axis=0, tiled=T...]
    ppermute x0 -> x7, starting transfers between devices: none -> 15.8 us  [the longest x3 12.6 us: ring_gather(): later.append(lax.ppermute(later[-1], axis, down))]
    ppermute x0 -> x7, waiting for transfers between devices: none -> 9.31 us  [the longest x4 9.31 us: ring_gather(): earlier.append(lax.ppermute(earlier[-1], axis, up))]
    unnamed x75 -> x98, local copies, waits for them, and re-layouts: 24.9 us -> 33.9 us
  transfers between devices with their start and end apart: 14 -> 21, of which waited for: 10 -> 14; matrix products, arithmetic and copies ran while one was open for 12% -> 12% of each run, Pallas kernels for 0% -> 0%
where the time goes in v1:
time: 807 us; the launch traced here: 796 us
  waiting for transfers between devices  380 us (47%)
  blocking collectives  149 us (18%)
  matrix products  115 us (14%)
  local copies, waits for them, and re-layouts  62.5 us (8%)
  other arithmetic  53.8 us (7%)
  between operations  17.7 us (2%)
  starting transfers between devices  17.4 us (2%)
    reduce_scatter x1, waiting for transfers between devices, body(): lax.psum_scatter(up_grad, 'dp', scatter_dimension=0, tiled=True)  73 us
    reduce_scatter x1, waiting for transfers between devices, body(): lax.psum_scatter(down_grad, 'dp', scatter_dimension=1, tiled=True)  70.9 us
    psum x1, blocking collectives, body(): lax.psum((spread(query_bias_part), spread(value_bias_part), spread(up_bia...  42.1 us
    pmax x1, blocking collectives, body(): lax.pmax((jnp.max(jnp.abs(inputs)), jnp.max(jnp.abs(context)), jnp.max(jn...  39.3 us
    reduce_scatter x1, waiting for transfers between devices, body(): lax.psum_scatter(matmul_right_t(grad_up, up_back).astype(jnp.bfloat16), '...  37.8 us
    reduce_scatter x1, waiting for transfers between devices, body(): lax.psum_scatter(jnp.einsum('jte,jde->td', stacked, qkv_back, preferred_e...  37 us
    all_gather x1, blocking collectives, body(): lax.all_gather(masters[0], 'dp', axis=1, tiled=True)  36.5 us
    reduce_scatter x1, waiting for transfers between devices, body(): lax.psum_scatter(matmul_plain(act_clip, down_full).astype(jnp.bfloat16),...  35.7 us
  transfers between devices with their start and end apart: 21, of which 14 were waited for; matrix products, arithmetic and copies ran while one was open for 12% of the time, Pallas kernels for 0%

profile of v1, /device:TPU:0, one launch (start us, length us, event | category | flops | bytes accessed | tf_op | source)
XLA Modules:
  0.0 796.1 jit_solution(3589021952459809245)
XLA Ops:
  10.0 2.8 fusion.80
  13.9 3.0 collective-permute-start
  16.9 3.1 collective-permute-start.4
  21.3 36.5 %all_gather.28 = bf16[3,768,192]{2,0,1:T(4,128)(2,1)S(1)} all-gather(bf16[3,96,192]{2,0,1:T(4,128)(2,1)S(1)} %copy.88), channel_id=1, replica_groups=mesh['dp'=8,'tensor'=4] {'dp'}, dimensions={1}, use_global_device_ids=true | all-gather | bytes 995328 | tf_op jit(solution)/shard_map/all_gather | solution.py:169
  58.6 6.4 collective-permute-done.1
  65.0 4.8 collective-permute-start.5
  72.9 4.8 collective-permute-start.6
  88.6 3.9 fusion.106
  94.0 3.2 squeeze.75
  97.1 2.2 squeeze.76
  100.1 2.9 fusion.83
  103.0 16.9 %while.26 = (s32[]{:T(128)}, f32[4,512,3,64]{1,3,2,0:T(8,128)}, f32[4,3,512]{2,1,0:T(4,128)}, bf16[4,512,3,64]{1,3,2,0:T(8,128)(2,1)S(1)}, s32[4,512]{1,0:T(4,12...) while((s32[]{:T(128)}, f32[4,512,3,64]{1,3,2,0:T(8,128)}, ...), condition=%wide.region_3.4_spmd, body=%wide.region_0.3_spmd.sunk | while | flops 211286528 | bytes 11534437 | solution.py:182
  119.9 4.2 abs_reduce_fusion.2
  125.7 3.7 convolution_convert_fusion.2
  131.4 34.8 %reduce-scatter.13.cloned.1.call-done = bf16[512,768]{1,0:T(8,128)(2,1)} async-done(((bf16[2048,768]{1,0:T(8,128)(2,1)}), bf16[512,768]{1,0:T(8,128)(2,1)}) %reduce-scatter.13.cloned.1.call-update) | async-done | bytes 786448 | tf_op jit(solution)/shard_map/reduce_scatter | solution.py:185
  169.4 2.2 multiply_convert_fusion.2
  172.8 28.8 %all-gather.9.cloned.1.call-done = bf16[2048,768]{1,0:T(8,128)(2,1)} async-done(((bf16[512,768]{1,0:T(8,128)(2,1)}), bf16[2048,768]{1,0:T(8,128)(2,1)}) %all-gather.9.cloned.1.call-update) | async-done | bytes 3145744 | tf_op jit(solution)/shard_map/all_gather | solution.py:194
  201.6 17.8 %abs_reduce_fusion = (f32[]{:T(128)}, f32[2048,768]{1,0:T(8,128)S(1)}, f32[2048,768]{1,0:T(8,128)}) fusion(f32[768]{0:T(1024)S(1)} %copy-done.34, bf16[2048,768]{1,0:T(8,128)(2,1)} %all-gather.9.cloned.1.call-done, bf16[768,768]{1,0:T(8,128)(2,1)} %all-gather.11.cloned.1.call-done), kind=kOutput, calls=%fused_computation.74 | convolution fusion | flops 2521300992 | bytes 16911364 | tf_op jit(solution)/shard_map/dot_general | solution.py:29
  219.4 2.7 copy-done.7
  222.1 3.6 multiply_convert_fusion.1
  225.7 20.0 %all-gather.13.cloned.1.call-done = bf16[768,768]{0,1:T(8,128)(2,1)} async-done(((bf16[768,96]{0,1:T(8,128)(2,1)}), bf16[768,768]{0,1:T(8,128)(2,1)}) %all-gather.13.cloned.1.call-update) | async-done | bytes 1179664 | tf_op jit(solution)/shard_map/all_gather | solution.py:172
  245.7 6.5 convolution_convert_fusion.1
  252.7 35.7 %reduce-scatter.15.cloned.1.call-done = bf16[512,768]{1,0:T(8,128)(2,1)} async-done(((bf16[2048,768]{1,0:T(8,128)(2,1)}), bf16[512,768]{1,0:T(8,128)(2,1)}) %reduce-scatter.15.cloned.1.call-update) | async-done | bytes 786448 | tf_op jit(solution)/shard_map/reduce_scatter | solution.py:198
  292.1 2.1 fusion.100
  296.5 28.6 %all-gather.15.cloned.1.call-done = bf16[2048,768]{1,0:T(8,128)(2,1)} async-done(((bf16[512,768]{1,0:T(8,128)(2,1)}), bf16[2048,768]{1,0:T(8,128)(2,1)}) %all-gather.15.cloned.1.call-update) | async-done | bytes 3145744 | tf_op jit(solution)/shard_map/all_gather | solution.py:219
  325.1 11.1 %convert_reduce_fusion = (f32[768]{0:T(1024)}, bf16[2048,768]{1,0:T(8,128)(2,1)S(1)}) fusion(f32[2048,768]{1,0:T(8,128)} %get-tuple-element.347, f32[768]{0:T(1024)S(1)} %copy-done.34, f32[2048,768]{1,0:T(8,128)} %copy-done.7, f32[]{:T(128)} %bitcast.27, bf16[2048,768]{1,0:T(8,128)(2,1)} %all-gather.15.cloned.1.call-done, ...), kind=kOutput, calls=%fused_computation.75 | convolution fusion | flops 2442657024 | bytes 20060164 | tf_op jit(solution)/shard_map/dot_general | solution.py:39
  337.8 4.0 convolution_convert_fusion
  341.9 37.8 %reduce-scatter.17.cloned.1.call-done = bf16[512,768]{1,0:T(8,128)(2,1)} async-done(((bf16[2048,768]{1,0:T(8,128)(2,1)}), bf16[512,768]{1,0:T(8,128)(2,1)}) %reduce-scatter.17.cloned.1.call-update) | async-done | bytes 786448 | tf_op jit(solution)/shard_map/reduce_scatter | solution.py:230
  379.7 4.8 multiply_reduce_fusion.1
  388.2 31.5 %all_gather.34 = bf16[192,768]{0,1:T(8,128)(2,1)S(1)} all-gather(bf16[192,96]{0,1:T(8,128)(2,1)S(1)} %copy-done.15), channel_id=1, replica_groups=mesh['dp'=8,'tensor'=4] {'dp'}, dimensions={1}, use_global_device_ids=true | all-gather | bytes 331776 | tf_op jit(solution)/shard_map/all_gather | solution.py:222
  419.7 2.4 copy.95
  423.8 3.5 fusion.70
  430.2 32.6 %while.27 = (s32[]{:T(128)}, bf16[4,512,3,64]{1,3,2,0:T(8,128)(2,1)}, bf16[4,512,3,64]{1,3,2,0:T(8,128)(2,1)}, bf16[4,512,3,64]{1,3,2,0:T(8,128)(2,1)}, bf16[4,5...) while((s32[]{:T(128)}, ...), condition=%wide.region_17.18_spmd, body=%wide.region_15.17_spmd.sunk | while | flops 511408640 | bytes 26129024 | solution.py:245
  465.2 4.2 convolution_bitcast_fusion
  476.1 4.6 fusion.85
  480.7 2.8 copy.107
  483.5 4.8 reshape.286
  488.4 6.1 bitcast_convert_fusion
  494.5 7.0 fusion.108
  501.9 7.0 fusion.107
  509.1 39.3 %all-reduce.2 = (f32[1]{0:T(128)}, f32[1]{0:T(128)}, f32[1]{0:T(128)}, f32[1]{0:T(128)}) all-reduce(f32[1]{0:T(128)} %bitcast.37, f32[1]{0:T(128)} %bitcast.36, f32[1]{0:T(128)} %bitcast.35, f32[1]{0:T(128)} %bitcast.34), channel_id=1, replica_groups=mesh['dp'=8,'tensor'=4] {'dp','tensor'}, use_global_device_ids=true, to_apply=%region_43.44 | all-reduce | flops 4 | bytes 32 | tf_op jit(solution)/shard_map/pmax | solution.py:206
  548.5 3.2 fusion.97
  553.6 42.1 %all-reduce.1 = (f32[768]{0:T(1024)S(1)}, f32[768]{0:T(1024)S(1)}, f32[6,768]{1,0:T(8,128)S(1)}, f32[3072]{0:T(1024)S(1)}) all-reduce(f32[768]{0:T(1024)S(1)} %mul.307, f32[768]{0:T(1024)S(1)} %mul.302, f32[6,768]{1,0:T(8,128)S(1)} %stack.58, f32[3072]{0:T(1024)S(1)} %mul.313), channel_id=1, replica_groups=mesh['dp'=8,'tensor'=4] {'dp','tensor'}, use_global_device_ids=true, to_apply=%region_23.24 | all-reduce | flops 9216 | bytes 73728 | tf_op jit(solution)/shard_map/psum | solution.py:292
  599.4 3.5 reduce-scatter.25.cloned.1.call-done
  604.8 37.0 %reduce-scatter.19.cloned.1.call-done = bf16[512,768]{1,0:T(8,128)(2,1)} async-done(((bf16[2048,768]{1,0:T(8,128)(2,1)}), bf16[512,768]{1,0:T(8,128)(2,1)}) %reduce-scatter.19.cloned.1.call-update) | async-done | bytes 786448 | tf_op jit(solution)/shard_map/reduce_scatter | solution.py:257
  641.8 2.9 add_convert_fusion
  644.7 70.9 %reduce-scatter.23.cloned.1.call-done = f32[768,96]{0,1:T(8,128)} async-done(((f32[768,768]{0,1:T(8,128)}), f32[768,96]{0,1:T(8,128)}) %reduce-scatter.23.cloned.1.call-update) | async-done | bytes 294928 | tf_op jit(solution)/shard_map/reduce_scatter | solution.py:272
  715.5 73.0 %reduce-scatter.21.cloned.1.call-done = f32[96,768]{1,0:T(8,128)} async-done(((f32[768,768]{1,0:T(8,128)}), f32[96,768]{1,0:T(8,128)}) %reduce-scatter.21.cloned.1.call-update) | async-done | bytes 294928 | tf_op jit(solution)/shard_map/reduce_scatter | solution.py:271
  (279 shorter events, 110.6 us)
Async XLA Ops:
  8.0 13.1 %copy-start.32 = (s32[12]{0:T(128)S(1)}, s32[12]{0:T(128)}, u32[]{:S(2)}) copy-start(s32[12]{0:T(128)} %param.37) | copy-start | bytes 148
  8.0 49.8 %copy-start.31 = (f32[2,192]{1,0:T(2,128)S(1)}, f32[2,192]{1,0:T(2,128)}, u32[]{:S(2)}) copy-start(f32[2,192]{1,0:T(2,128)} %param.24) | copy-start | bytes 4612
  8.0 80.5 %all-gather.7.cloned.1.call-start = ((), (), s32[]{:S(2)}) async-start(), calls=%async_computation.8 | async-start | bytes 3932160 | tf_op jit(solution)/shard_map/all_gather | solution.py:176
  12.8 153.4 %reduce-scatter.13.cloned.1.call-start = ((), (), s32[]{:S(2)}) async-start(), calls=%async_computation.9 | async-start | bytes 3932160 | tf_op jit(solution)/shard_map/reduce_scatter | solution.py:185
  13.9 72.2 %copy-start.14 = (bf16[192,96]{0,1:T(8,128)(2,1)}, bf16[192,96]{0,1:T(8,128)(2,1)S(1)}, u32[]{:S(2)}) copy-start(bf16[192,96]{0,1:T(8,128)(2,1)S(1)} %copy.94) | copy-start | bytes 110596
  13.9 44.0 %collective-permute-start = (bf16[192,96]{0,1:T(8,128)(2,1)S(1)}, bf16[192,96]{0,1:T(8,128)(2,1)S(1)}, u32[]{:S(2)}, u32[]{:S(2)}) collective-permute-start(bf16[192,96]{0,1:T(8,128)(2,1)S(1)} %copy.94), channel_id=1, source_target_pairs={{0,4},{4,8},{8,12},{12,16},{16,20},{20,24},{24,28},{28,0},{1,5},{5... | collective-permute-start | bytes 110600 | tf_op jit(solution)/shard_map/ppermute | solution.py:21
  16.9 48.1 %collective-permute-start.4 = (bf16[192,96]{0,1:T(8,128)(2,1)S(1)}, bf16[192,96]{0,1:T(8,128)(2,1)S(1)}, u32[]{:S(2)}, u32[]{:S(2)}) collective-permute-start(bf16[192,96]{0,1:T(8,128)(2,1)S(1)} %copy.94), channel_id=1, source_target_pairs={{0,28},{4,0},{8,4},{12,8},{16,12},{20,16},{24,20},{28,24},{1,29},{... | collective-permute-start | bytes 110600 | tf_op jit(solution)/shard_map/ppermute | solution.py:23
  57.8 7.2 collective-permute-start.1
  65.0 6.8 collective-permute-start.2
  65.0 7.9 collective-permute-start.5
  71.8 6.8 collective-permute-start.3
  72.7 19.8 %copy-start.11 = (bf16[3,768,192]{1,2,0:T(8,128)(2,1)}, bf16[3,768,192]{1,2,0:T(8,128)(2,1)S(1)}, u32[]{:S(2)}) copy-start(bf16[3,768,192]{1,2,0:T(8,128)(2,1)S(1)} %copy.89) | copy-start | bytes 2654212
  72.9 10.0 %collective-permute-start.6 = (bf16[192,96]{0,1:T(8,128)(2,1)S(1)}, bf16[192,96]{0,1:T(8,128)(2,1)S(1)}, u32[]{:S(2)}, u32[]{:S(2)}) collective-permute-start(bf16[192,96]{0,1:T(8,128)(2,1)S(1)} %collective-permute-done.5), channel_id=1, source_target_pairs={{0,28},{4,0},{8,4},{12,8},{16,12},{20,16},{24,20},{28,24},{1,29},{... | collective-permute-start | bytes 110600 | tf_op jit(solution)/shard_map/ppermute | solution.py:23
  119.9 5.0 copy-start.8
  129.5 36.8 %copy-start = (bf16[512,768]{1,0:T(8,128)(2,1)S(1)}, bf16[512,768]{1,0:T(8,128)(2,1)}, u32[]{:S(2)}) copy-start(bf16[512,768]{1,0:T(8,128)(2,1)} %param.21) | copy-start | bytes 2359300
  129.5 36.8 %copy-start.18 = (f32[768]{0:T(1024)S(1)}, f32[768]{0:T(1024)}, u32[]{:S(2)}) copy-start(f32[768]{0:T(1024)} %param.26) | copy-start | bytes 9220
  129.5 39.9 %copy-start.19 = (f32[768]{0:T(1024)S(1)}, f32[768]{0:T(1024)}, u32[]{:S(2)}) copy-start(f32[768]{0:T(1024)} %param.27) | copy-start | bytes 9220
  129.5 39.9 %copy-start.20 = (f32[768]{0:T(1024)S(1)}, f32[768]{0:T(1024)}, u32[]{:S(2)}) copy-start(f32[768]{0:T(1024)} %param.28) | copy-start | bytes 9220
  129.5 43.3 %all-gather.11.cloned.1.call-start = ((), (), s32[]{:S(2)}) async-start(), calls=%async_computation.11 | async-start | bytes 1327104 | tf_op jit(solution)/shard_map/all_gather | solution.py:171
  131.1 40.5 %copy-start.17 = (f32[768,96]{0,1:T(8,128)S(1)}, f32[768,96]{0,1:T(8,128)}, u32[]{:S(2)}) copy-start(f32[768,96]{0,1:T(8,128)} %param.31) | copy-start | bytes 884740
  131.1 70.4 %copy-start.34 = (f32[768]{0:T(1024)S(1)}, f32[768]{0:T(1024)}, u32[]{:S(2)}) copy-start(f32[768]{0:T(1024)} %param.30) | copy-start | bytes 9220
  131.2 70.4 %all-gather.9.cloned.1.call-start = ((), (), s32[]{:S(2)}) async-start(), calls=%async_computation.10 | async-start | bytes 3932160 | tf_op jit(solution)/shard_map/all_gather | solution.py:194
  166.3 3.2 copy-start.1
  171.6 74.0 %all-gather.13.cloned.1.call-start = ((), (), s32[]{:S(2)}) async-start(), calls=%async_computation.12 | async-start | bytes 1327104 | tf_op jit(solution)/shard_map/all_gather | solution.py:172
  172.4 116.0 %reduce-scatter.15.cloned.1.call-start = ((), (), s32[]{:S(2)}) async-start(), calls=%async_computation.13 | async-start | bytes 3932160 | tf_op jit(solution)/shard_map/reduce_scatter | solution.py:198
  252.2 36.2 %copy-start.29 = (f32[768]{0:T(1024)S(1)}, f32[768]{0:T(1024)}, u32[]{:S(2)}) copy-start(f32[768]{0:T(1024)} %param.32) | copy-start | bytes 9220
  252.2 38.5 %copy-start.22 = (f32[768]{0:T(1024)S(1)}, f32[768]{0:T(1024)}, u32[]{:S(2)}) copy-start(f32[768]{0:T(1024)} %param.33) | copy-start | bytes 9220
  252.2 39.8 %copy-start.30 = (f32[768]{0:T(1024)S(1)}, f32[768]{0:T(1024)}, u32[]{:S(2)}) copy-start(f32[768]{0:T(1024)} %param.34) | copy-start | bytes 9220
  252.2 72.8 %all-gather.15.cloned.1.call-start = ((), (), s32[]{:S(2)}) async-start(), calls=%async_computation.14 | async-start | bytes 3932160 | tf_op jit(solution)/shard_map/all_gather | solution.py:219
  296.4 83.3 %reduce-scatter.17.cloned.1.call-start = ((), (), s32[]{:S(2)}) async-start(), calls=%async_computation.15 | async-start | bytes 3932160 | tf_op jit(solution)/shard_map/reduce_scatter | solution.py:230
  325.1 12.7 %copy-start.33 = (bf16[768,768]{1,0:T(8,128)(2,1)S(1)}, bf16[768,768]{1,0:T(8,128)(2,1)}, u32[]{:S(2)}) copy-start(bf16[768,768]{1,0:T(8,128)(2,1)} %all-gather.11.cloned.1.call-done) | copy-start | bytes 3538948
  341.9 82.0 %all-gather.17.cloned.1.call-start = ((), (), s32[]{:S(2)}) async-start(), calls=%async_computation.16 | async-start | bytes 3932160 | tf_op jit(solution)/shard_map/all_gather | solution.py:240
  388.1 209.6 %reduce-scatter.27.cloned.1.call-start = ((), (), s32[]{:S(2)}) async-start(), calls=%async_computation.21 | async-start | bytes 884736
  465.2 5.4 copy-start.13
  469.5 133.4 %reduce-scatter.25.cloned.1.call-start = ((), (), s32[]{:S(2)}) async-start(), calls=%async_computation.20 | async-start | bytes 2211840
  483.5 4.9 copy-start.12
  488.3 153.5 %reduce-scatter.19.cloned.1.call-start = ((), (), s32[]{:S(2)}) async-start(), calls=%async_computation.17 | async-start | bytes 3932160 | tf_op jit(solution)/shard_map/reduce_scatter | solution.py:257
  494.5 221.1 %reduce-scatter.23.cloned.1.call-start = ((), (), s32[]{:S(2)}) async-start(), calls=%async_computation.19 | async-start | bytes 2654208 | tf_op jit(solution)/shard_map/reduce_scatter | solution.py:272
  501.5 7.4 copy-start.23
  501.5 7.5 copy-start.21
  501.5 7.5 copy-start.28
  501.5 46.9 %copy-start.26 = (f32[768]{0:T(1024)S(1)}, f32[768]{0:T(1024)}, u32[]{:S(2)}) copy-start(f32[768]{0:T(1024)} %get-tuple-element.326) | copy-start | bytes 9220
  501.5 46.9 %copy-start.25 = (f32[768]{0:T(1024)S(1)}, f32[768]{0:T(1024)}, u32[]{:S(2)}) copy-start(f32[768]{0:T(1024)} %get-tuple-element.258) | copy-start | bytes 9220
  501.6 46.9 %copy-start.24 = (f32[768]{0:T(1024)S(1)}, f32[768]{0:T(1024)}, u32[]{:S(2)}) copy-start(f32[768]{0:T(1024)} %get-tuple-element.264) | copy-start | bytes 9220
  501.6 47.0 %copy-start.27 = (f32[4]{0:T(128)S(1)}, f32[4]{0:T(128)}, u32[]{:S(2)}) copy-start(f32[4]{0:T(128)} %param.35) | copy-start | bytes 52
  501.6 50.1 %copy-start.9 = (bf16[4,512,3,64]{1,3,2,0:T(8,128)(2,1)S(1)}, bf16[4,512,3,64]{1,3,2,0:T(8,128)(2,1)}, u32[]{:S(2)}) copy-start(bf16[4,512,3,64]{1,3,2,0:T(8,128)(2,1)} %get-tuple-element.119) | copy-start | bytes 2359300
  501.6 287.0 %reduce-scatter.21.cloned.1.call-start = ((), (), s32[]{:S(2)}) async-start(), calls=%async_computation.18 | async-start | bytes 2654208 | tf_op jit(solution)/shard_map/reduce_scatter | solution.py:271
  508.9 132.9 %copy-start.3 = (f32[512,768]{1,0:T(8,128)S(1)}, f32[512,768]{1,0:T(8,128)}, u32[]{:S(2)}) copy-start(f32[512,768]{1,0:T(8,128)} %copy-done.2) | copy-start | bytes 4718596
  (9 other events, 15.7 us)
Sparse Core Ops, SparseCore 0:
  12.9 31.2 all-gather.6
  129.6 36.5 reduce-scatter.12
  296.5 28.5 all-gather.14
  388.2 28.4 all-gather.16
Sparse Core Ops, SparseCore 1:
  132.8 40.0 all-gather.10
  174.8 26.7 all-gather.8
  204.2 41.4 all-gather.12
  252.3 36.0 reduce-scatter.14
  342.0 37.7 reduce-scatter.16
  469.5 63.2 reduce-scatter.26
  536.2 66.6 reduce-scatter.24
  605.3 36.4 reduce-scatter.18
  645.7 69.8 reduce-scatter.22
  719.6 68.9 reduce-scatter.20
